TPU v7x, 32 devices: a whole 2x2x4 slice. The times are simulated.
32 devices in a mesh: groups: 2 (over y), ctx: 16 (over z, x, core).
Axes of the slice: x: 2, y: 2, z: 4, core: 2. Of those that a mesh axis runs over, the one named last changes fastest.
Arguments:
- queries: bfloat16 [16384, 2048], P(('groups', 'ctx')), parts along dimension 0, may hold values from -60 to 60
- keys: bfloat16 [16384, 512], P(('groups', 'ctx')), parts along dimension 0, may hold values from -30 to 30
- values: bfloat16 [16384, 512], P(('groups', 'ctx')), parts along dimension 0, may hold values from -24 to 24
- block_lengths: int32 [32], P(('groups', 'ctx')), parts along dimension 0, may hold values from 256 to 512, as said below
- out_weight: bfloat16 [2048, 4096], P(None, 'ctx'), may hold values from -0.125 to 0.125
Outputs:
- hidden_states: bfloat16 [16384, 4096], P(('groups', 'ctx')), parts along dimension 0
There are 2 independent parts, one for each index of `groups`. A program takes and returns all parts, laid end to end along the dimension named above; an argument that names none is the same for every part. Nothing has to cross between parts.
Inputs may be any that keep to these rules, and one draw needn't show every extreme that they name: `block_lengths`: block 0 always holds 512 valid tokens.
All inputs are finite; a program needn't handle non-finite values.
Results may differ from a plain program's by a relative error of at most 0.0057.
Values may be sent and summed in bfloat16 or wider, within the bound.
A program may use at most 128 MiB of HBM per device.

v0:
```python
import math
import jax
import jax.numpy as jnp
from jax import lax
from jax.sharding import PartitionSpec as P

HD = 128


def broadcast(block, axis, source):
    block = jnp.where(lax.axis_index(axis) == source, block, jnp.zeros_like(block))
    return lax.psum(block, axis)


def make_mask(row_count, valid_length, has_anchor):
    row_ids = jnp.arange(row_count)[:, None]
    col_ids = jnp.arange(row_count)[None, :]
    local_mask = (col_ids <= row_ids) & (col_ids < valid_length)
    anchor_mask = jnp.broadcast_to(has_anchor, (row_count, row_count))
    return jnp.concatenate([anchor_mask, local_mask], axis=1)


def attend(query_rows, key_rows, value_rows, anchor_keys, anchor_values, valid_length, has_anchor):
    row_count = query_rows.shape[0]
    key_heads = key_rows.shape[1] // HD
    group_size = query_rows.shape[1] // key_rows.shape[1]
    query_stack = query_rows.reshape(row_count, key_heads, group_size, HD).transpose(1, 0, 2, 3)
    key_stack = (
        jnp.concatenate([anchor_keys, key_rows], axis=0)
        .reshape(2 * row_count, key_heads, HD)
        .transpose(1, 0, 2)
    )
    value_stack = (
        jnp.concatenate([anchor_values, value_rows], axis=0)
        .reshape(2 * row_count, key_heads, HD)
        .transpose(1, 0, 2)
    )
    visible = make_mask(row_count, valid_length, has_anchor)

    def one_head(operands):
        head_queries, head_keys, head_values = operands
        scores = jnp.einsum(
            "qgd,kd->gqk", head_queries, head_keys, preferred_element_type=jnp.float32
        ) / math.sqrt(HD)
        scores = jnp.where(visible[None], scores, -jnp.inf)
        row_top = jnp.max(scores, axis=-1, keepdims=True)
        exponent = jnp.exp(scores - row_top)
        soft_weights = (exponent / jnp.sum(exponent, axis=-1, keepdims=True)).astype(jnp.bfloat16)
        mixture = jnp.einsum(
            "gqk,kd->qgd", soft_weights, head_values, preferred_element_type=jnp.float32
        )
        return mixture.astype(jnp.bfloat16)

    stacked = lax.map(one_head, (query_stack, key_stack, value_stack))
    return stacked.transpose(1, 0, 2, 3).reshape(row_count, key_heads * group_size * HD)


def per_device(queries, keys, values, block_lengths, out_weight):
    has_anchor = lax.axis_index("ctx") > 0
    anchor_keys, anchor_values = (broadcast(keys, "ctx", 0), broadcast(values, "ctx", 0))
    mixture = attend(
        queries, keys, values, anchor_keys, anchor_values, block_lengths[0], has_anchor
    )
    output = jnp.dot(
        mixture,
        lax.all_gather(out_weight, "ctx", axis=1, tiled=True),
        preferred_element_type=jnp.float32,
    )
    return output.astype(jnp.bfloat16)


def solution(mesh):
    return jax.shard_map(
        per_device,
        mesh=mesh,
        in_specs=(
            P(("groups", "ctx"), None),
            P(("groups", "ctx"), None),
            P(("groups", "ctx"), None),
            P(("groups", "ctx")),
            P(None, "ctx"),
        ),
        out_specs=P(("groups", "ctx"), None),
        check_vma=False,
    )
```

profile of v0, /device:TPU:0, one launch (start us, length us, event | category | flops | bytes accessed | tf_op | source)
XLA Modules:
  0.0 260.0 jit_solution(13996809299489624549)
XLA Ops:
  6.5 0.0 copy-start
  6.5 0.0 all-reduce.4.cloned.1.call-start
  6.5 1.4 copy.11
  7.9 1.3 copy.9
  9.2 1.1 broadcast_select_fusion
  10.3 0.0 all-reduce.4.cloned.1.call-update
  10.3 0.0 all-gather.2.cloned.1.call-start
  10.4 0.7 all-gather.2.cloned.1.call-update
  11.7 0.0 copy-done
  11.7 2.5 copy.13
  14.3 0.1 fusion.39
  14.4 0.9 concatenate.10
  15.3 91.5 %all-reduce.4.cloned.1.call-done = (bf16[512,512]{0,1:T(8,128)(2,1)}, bf16[512,512]{0,1:T(8,128)(2,1)}) async-done(((bf16[512,512]{0,1:T(8,128)(2,1)}, bf16[512,512]{0,1:T(8,128)(2,1)}), (bf16[512,512]{0,1:T(8,128)(2,1)}, bf16[512,512]{0,1:T(8,128)(2,1)})) %all-reduce.4.cloned.1.call-update) | async-done | bytes 1048592 | tf_op jit(solution)/shard_map/psum | solution.py:12
  106.8 1.2 pad_maximum_fusion.1
  108.0 1.2 pad_maximum_fusion
  109.2 50.2 %while.10 = (s32[]{:T(128)}, bf16[4,512,4,128]{1,3,2,0:T(8,128)(2,1)}, bf16[4,1024,128]{1,2,0:T(8,128)(2,1)S(1)}, pred[512,1024]{0,1:T(8,128)(4,1)}, bf16[4,1024...) while((s32[]{:T(128)}, bf16[4,512,4,128]{1,3,2,0:T(8,128)(2,1)}, ...), condition=%wide.region_5.6_spmd, body=%wide.region_2.5_spmd.sunk | while | flops 1086587904 | bytes 18892876 | solution.py:54
  109.2 7.8 %fusion.59 = (f32[4,512]{1,0:T(4,128)S(1)}, f32[4,512,1024]{1,2,0:T(8,128)}) fusion(pred[512,1024]{0,1:T(8,128)(4,1)} %get-tuple-element.120, bf16[4,512,4,128]{1,3,2,0:T(8,128)(2,1)} %get-tuple-element.122, s32[]{:T(128)} %get-tuple-element.110, bf16[4,1024,128]{1,2,0:T(8,128)(2,1)S(1)} %get-tuple-element.121), kind=kOutput, calls=%fused_computation.37.clone.1 | convolution fusion | flops 545260544 | bytes 9708544 | tf_op jit(solution)/shard_map/while/body/eval_jaxpr/sub | solution.py:47
  117.0 5.3 %fusion.60 = bf16[4,512,4,128]{1,3,2,0:T(8,128)(2,1)} fusion(bf16[4,512,4,128]{1,3,2,0:T(8,128)(2,1)} %get-tuple-element.111, s32[]{:T(128)} %get-tuple-element.110, f32[4,512,1024]{1,2,0:T(8,128)} %get-tuple-element.101, f32[4,512]{1,0:T(4,128)S(1)} %get-tuple-element.102, bf16[4,1024,128]{1,2,0:T(8,128)(2,1)S(1)} %get-tuple-element.119), kind=kOutput, calls=%fused_computation.11.clone.1 | convolution fusion | flops 541327360 | bytes 9184256 | tf_op jit(solution)/shard_map/while/body/eval_jaxpr/gqk,kd->qgd/dot_general | solution.py:49
  122.2 7.5 %fusion.59 = (f32[4,512]{1,0:T(4,128)S(1)}, f32[4,512,1024]{1,2,0:T(8,128)}) fusion(pred[512,1024]{0,1:T(8,128)(4,1)} %get-tuple-element.120, bf16[4,512,4,128]{1,3,2,0:T(8,128)(2,1)} %get-tuple-element.122, s32[]{:T(128)} %get-tuple-element.110, bf16[4,1024,128]{1,2,0:T(8,128)(2,1)S(1)} %get-tuple-element.121), kind=kOutput, calls=%fused_computation.37.clone.1 | convolution fusion | flops 545260544 | bytes 9708544 | tf_op jit(solution)/shard_map/while/body/eval_jaxpr/sub | solution.py:47
  129.7 5.0 %fusion.60 = bf16[4,512,4,128]{1,3,2,0:T(8,128)(2,1)} fusion(bf16[4,512,4,128]{1,3,2,0:T(8,128)(2,1)} %get-tuple-element.111, s32[]{:T(128)} %get-tuple-element.110, f32[4,512,1024]{1,2,0:T(8,128)} %get-tuple-element.101, f32[4,512]{1,0:T(4,128)S(1)} %get-tuple-element.102, bf16[4,1024,128]{1,2,0:T(8,128)(2,1)S(1)} %get-tuple-element.119), kind=kOutput, calls=%fused_computation.11.clone.1 | convolution fusion | flops 541327360 | bytes 9184256 | tf_op jit(solution)/shard_map/while/body/eval_jaxpr/gqk,kd->qgd/dot_general | solution.py:49
  134.7 7.5 %fusion.59 = (f32[4,512]{1,0:T(4,128)S(1)}, f32[4,512,1024]{1,2,0:T(8,128)}) fusion(pred[512,1024]{0,1:T(8,128)(4,1)} %get-tuple-element.120, bf16[4,512,4,128]{1,3,2,0:T(8,128)(2,1)} %get-tuple-element.122, s32[]{:T(128)} %get-tuple-element.110, bf16[4,1024,128]{1,2,0:T(8,128)(2,1)S(1)} %get-tuple-element.121), kind=kOutput, calls=%fused_computation.37.clone.1 | convolution fusion | flops 545260544 | bytes 9708544 | tf_op jit(solution)/shard_map/while/body/eval_jaxpr/sub | solution.py:47
  142.2 4.9 %fusion.60 = bf16[4,512,4,128]{1,3,2,0:T(8,128)(2,1)} fusion(bf16[4,512,4,128]{1,3,2,0:T(8,128)(2,1)} %get-tuple-element.111, s32[]{:T(128)} %get-tuple-element.110, f32[4,512,1024]{1,2,0:T(8,128)} %get-tuple-element.101, f32[4,512]{1,0:T(4,128)S(1)} %get-tuple-element.102, bf16[4,1024,128]{1,2,0:T(8,128)(2,1)S(1)} %get-tuple-element.119), kind=kOutput, calls=%fused_computation.11.clone.1 | convolution fusion | flops 541327360 | bytes 9184256 | tf_op jit(solution)/shard_map/while/body/eval_jaxpr/gqk,kd->qgd/dot_general | solution.py:49
  147.1 7.5 %fusion.59 = (f32[4,512]{1,0:T(4,128)S(1)}, f32[4,512,1024]{1,2,0:T(8,128)}) fusion(pred[512,1024]{0,1:T(8,128)(4,1)} %get-tuple-element.120, bf16[4,512,4,128]{1,3,2,0:T(8,128)(2,1)} %get-tuple-element.122, s32[]{:T(128)} %get-tuple-element.110, bf16[4,1024,128]{1,2,0:T(8,128)(2,1)S(1)} %get-tuple-element.121), kind=kOutput, calls=%fused_computation.37.clone.1 | convolution fusion | flops 545260544 | bytes 9708544 | tf_op jit(solution)/shard_map/while/body/eval_jaxpr/sub | solution.py:47
  154.6 4.9 %fusion.60 = bf16[4,512,4,128]{1,3,2,0:T(8,128)(2,1)} fusion(bf16[4,512,4,128]{1,3,2,0:T(8,128)(2,1)} %get-tuple-element.111, s32[]{:T(128)} %get-tuple-element.110, f32[4,512,1024]{1,2,0:T(8,128)} %get-tuple-element.101, f32[4,512]{1,0:T(4,128)S(1)} %get-tuple-element.102, bf16[4,1024,128]{1,2,0:T(8,128)(2,1)S(1)} %get-tuple-element.119), kind=kOutput, calls=%fused_computation.11.clone.1 | convolution fusion | flops 541327360 | bytes 9184256 | tf_op jit(solution)/shard_map/while/body/eval_jaxpr/gqk,kd->qgd/dot_general | solution.py:49
  159.4 79.2 %all-gather.2.cloned.1.call-done = bf16[2048,4096]{1,0:T(8,128)(2,1)} async-done(((bf16[2048,256]{1,0:T(8,128)(2,1)}), bf16[2048,4096]{1,0:T(8,128)(2,1)}) %all-gather.2.cloned.1.call-update) | async-done | bytes 16777232 | tf_op jit(solution)/shard_map/all_gather | solution.py:66
  238.7 14.5 %convolution_convert_fusion = bf16[512,4096]{1,0:T(8,128)(2,1)} fusion(bf16[512,2048]{0,1:T(8,128)(2,1)} %bitcast.77, bf16[2048,4096]{1,0:T(8,128)(2,1)} %all-gather.2.cloned.1.call-done), kind=kOutput, calls=%fused_computation.29 | convolution fusion | flops 8592031744 | bytes 23068672 | tf_op jit(solution)/shard_map/dot_general | solution.py:64
  (2 shorter events, 0.0 us)
Async XLA Ops:
  6.5 5.2 %copy-start = (bf16[512,2048]{1,0:T(8,128)(2,1)S(1)}, bf16[512,2048]{1,0:T(8,128)(2,1)}, u32[]{:S(2)}) copy-start(bf16[512,2048]{1,0:T(8,128)(2,1)} %param.7) | copy-start | bytes 6291460
  6.5 100.3 %all-reduce.4.cloned.1.call-start = ((), (), s32[]{:S(2)}) async-start(), calls=%async_computation.1 | async-start | bytes 2097152 | tf_op jit(solution)/shard_map/psum | solution.py:12
  10.3 228.3 %all-gather.2.cloned.1.call-start = ((), (), s32[]{:S(2)}) async-start(), calls=%async_computation | async-start | bytes 17825792 | tf_op jit(solution)/shard_map/all_gather | solution.py:66
Sparse Core Ops, SparseCore 0:
  10.9 95.8 all-reduce.3
  109.0 129.6 all-gather.1
where the time goes:
time: 260 us
  waiting for transfers between devices  171 us (66%)
  matrix products  64.7 us (25%)
  between operations  14.1 us (5%)
  local copies, waits for them, and re-layouts  6.06 us (2%)
  other arithmetic  3.6 us (1%)
    psum x1, waiting for transfers between devices, broadcast(): return lax.psum(block, axis)  91.5 us
    all_gather x1, waiting for transfers between devices, per_device(): lax.all_gather(out_weight, 'ctx', axis=1, tiled=True)  79.2 us
    sub x4, matrix products, one_head(): exponent = jnp.exp(scores - row_top)  30.2 us
    dot_general x4, matrix products, one_head(): jnp.einsum('gqk,kd->qgd', soft_weights, head_values, preferred_element_ty...  20.1 us
    dot_general x1, matrix products, per_device(): jnp.dot(mixture, lax.all_gather(out_weight, 'ctx', axis=1, tiled=True), p...  14.5 us
  transfers between devices with their start and end apart: 2, of which 2 were waited for; matrix products, arithmetic and copies ran while one was open for 22% of the time, Pallas kernels for 0%

commit v1 on v0

--- a/solution.py
+++ b/solution.py
@@ -9,7 +9,7 @@
 
 def broadcast(block, axis, source):
     block = jnp.where(lax.axis_index(axis) == source, block, jnp.zeros_like(block))
-    return lax.psum(block, axis)
+    return jnp.sum(lax.all_gather(block, axis), axis=0)
 
 
 def make_mask(row_count, valid_length, has_anchor):

time: 260 us -> 315 us (1.21)
  waiting for transfers between devices: 171 us -> 217 us
  other arithmetic: 3.6 us -> 13.9 us
    all_gather x0 -> x2, waiting for transfers between devices: none -> 141 us  [broadcast(): return jnp.sum(lax.all_gather(block, axis), axis=0)]
    psum x1 -> x0, waiting for transfers between devices: 91.5 us -> none  [broadcast(): return lax.psum(block, axis)]
    reduce_sum x0 -> x2, other arithmetic: none -> 9.76 us  [broadcast(): return jnp.sum(lax.all_gather(block, axis), axis=0)]
    all_gather x1, waiting for transfers between devices: 79.2 us -> 74.6 us  [per_device(): lax.all_gather(out_weight, 'ctx', axis=1, tiled=True)]
  transfers between devices with their start and end apart: 2 -> 3, of which waited for: 2 -> 3; matrix products, arithmetic and copies ran while one was open for 22% -> 21% of each run, Pallas kernels for 0% -> 0%
where the time goes in v1:
time: 315 us; the launch traced here: 314 us
  waiting for transfers between devices  217 us (69%)
  matrix products  65.1 us (21%)
  other arithmetic  13.9 us (4%)
  between operations  13.8 us (4%)
  local copies, waits for them, and re-layouts  4.49 us (1%)
    all_gather x2, waiting for transfers between devices, broadcast(): return jnp.sum(lax.all_gather(block, axis), axis=0)  141 us
    all_gather x1, waiting for transfers between devices, per_device(): lax.all_gather(out_weight, 'ctx', axis=1, tiled=True)  74.6 us
    sub x4, matrix products, one_head(): exponent = jnp.exp(scores - row_top)  29.9 us
    dot_general x4, matrix products, one_head(): jnp.einsum('gqk,kd->qgd', soft_weights, head_values, preferred_element_ty...  20.8 us
    dot_general x1, matrix products, per_device(): jnp.dot(mixture, lax.all_gather(out_weight, 'ctx', axis=1, tiled=True), p...  14.5 us
    reduce_sum x2, other arithmetic, broadcast(): return jnp.sum(lax.all_gather(block, axis), axis=0)  9.76 us
  transfers between devices with their start and end apart: 3, of which 3 were waited for; matrix products, arithmetic and copies ran while one was open for 21% of the time, Pallas kernels for 0%

profile of v1, /device:TPU:0, one launch (start us, length us, event | category | flops | bytes accessed | tf_op | source)
XLA Modules:
  0.0 314.3 jit_solution(5116936803249667406)
XLA Ops:
  6.5 0.0 copy-start
  6.5 0.0 all-gather.8.cloned.1.call-start
  6.5 2.0 broadcast_select_fusion.1
  8.6 0.0 all-gather.8.cloned.1.call-update
  8.6 0.0 all-gather.10.cloned.1.call-start
  8.6 1.9 broadcast_select_fusion
  10.5 0.0 all-gather.10.cloned.1.call-update
  10.5 0.0 all-gather.6.cloned.1.call-start
  10.6 0.7 all-gather.6.cloned.1.call-update
  11.9 0.0 copy-done
  11.9 2.5 copy.17
  14.4 0.1 fusion.39
  14.6 0.9 concatenate.10
  15.5 71.7 %all-gather.8.cloned.1.call-done = bf16[8192,512]{1,0:T(8,128)(2,1)} async-done(((bf16[512,512]{1,0:T(8,128)(2,1)}), bf16[8192,512]{1,0:T(8,128)(2,1)}) %all-gather.8.cloned.1.call-update) | async-done | bytes 8388624 | tf_op jit(solution)/shard_map/all_gather | solution.py:12
  87.1 0.0 copy-start.1
  87.1 4.9 %reduce_sum.33 = bf16[512,512]{1,0:T(8,128)(2,1)S(1)} reduce(bf16[16,512,512]{2,1,0:T(8,128)(2,1)} %bitcast.76, bf16[]{:T(256)} %constant.29.clone.1), dimensions={0}, to_apply=%region_1.2 | reduce | flops 3932160 | bytes 8912898 | tf_op jit(solution)/shard_map/reduce_sum | solution.py:12
  92.0 0.0 copy-done.1
  92.0 0.1 pad_maximum_fusion
  92.1 0.5 copy.15
  92.7 69.8 %all-gather.10.cloned.1.call-done = bf16[8192,512]{1,0:T(8,128)(2,1)} async-done(((bf16[512,512]{1,0:T(8,128)(2,1)}), bf16[8192,512]{1,0:T(8,128)(2,1)}) %all-gather.10.cloned.1.call-update) | async-done | bytes 8388624 | tf_op jit(solution)/shard_map/all_gather | solution.py:12
  162.5 0.0 copy-start.2
  162.5 4.9 %reduce_sum.34 = bf16[512,512]{1,0:T(8,128)(2,1)S(1)} reduce(bf16[16,512,512]{2,1,0:T(8,128)(2,1)} %bitcast.77, bf16[]{:T(256)} %constant.29.clone.1), dimensions={0}, to_apply=%region_0.1 | reduce | flops 3932160 | bytes 8912898 | tf_op jit(solution)/shard_map/reduce_sum | solution.py:12
  167.4 0.0 copy-done.2
  167.4 0.1 pad_maximum_fusion.1
  167.5 0.5 copy.16
  168.0 50.7 %while.10 = (s32[]{:T(128)}, bf16[4,512,4,128]{1,3,2,0:T(8,128)(2,1)}, bf16[4,1024,128]{1,2,0:T(8,128)(2,1)S(1)}, pred[512,1024]{0,1:T(8,128)(4,1)}, bf16[4,1024...) while((s32[]{:T(128)}, bf16[4,512,4,128]{1,3,2,0:T(8,128)(2,1)}, ...), condition=%wide.region_5.6_spmd, body=%wide.region_2.5_spmd.sunk | while | flops 1086587904 | bytes 18892876 | solution.py:54
  168.0 7.5 %fusion.59 = (f32[4,512]{1,0:T(4,128)S(1)}, f32[4,512,1024]{1,2,0:T(8,128)}) fusion(pred[512,1024]{0,1:T(8,128)(4,1)} %get-tuple-element.122, bf16[4,512,4,128]{1,3,2,0:T(8,128)(2,1)} %get-tuple-element.124, s32[]{:T(128)} %get-tuple-element.112, bf16[4,1024,128]{1,2,0:T(8,128)(2,1)S(1)} %get-tuple-element.123), kind=kOutput, calls=%fused_computation.37.clone.1 | convolution fusion | flops 545260544 | bytes 9708544 | tf_op jit(solution)/shard_map/while/body/eval_jaxpr/sub | solution.py:47
  175.5 4.9 %fusion.60 = bf16[4,512,4,128]{1,3,2,0:T(8,128)(2,1)} fusion(bf16[4,512,4,128]{1,3,2,0:T(8,128)(2,1)} %get-tuple-element.113, s32[]{:T(128)} %get-tuple-element.112, f32[4,512,1024]{1,2,0:T(8,128)} %get-tuple-element.103, f32[4,512]{1,0:T(4,128)S(1)} %get-tuple-element.104, bf16[4,1024,128]{1,2,0:T(8,128)(2,1)S(1)} %get-tuple-element.121), kind=kOutput, calls=%fused_computation.11.clone.1 | convolution fusion | flops 541327360 | bytes 9184256 | tf_op jit(solution)/shard_map/while/body/eval_jaxpr/gqk,kd->qgd/dot_general | solution.py:49
  180.4 7.5 %fusion.59 = (f32[4,512]{1,0:T(4,128)S(1)}, f32[4,512,1024]{1,2,0:T(8,128)}) fusion(pred[512,1024]{0,1:T(8,128)(4,1)} %get-tuple-element.122, bf16[4,512,4,128]{1,3,2,0:T(8,128)(2,1)} %get-tuple-element.124, s32[]{:T(128)} %get-tuple-element.112, bf16[4,1024,128]{1,2,0:T(8,128)(2,1)S(1)} %get-tuple-element.123), kind=kOutput, calls=%fused_computation.37.clone.1 | convolution fusion | flops 545260544 | bytes 9708544 | tf_op jit(solution)/shard_map/while/body/eval_jaxpr/sub | solution.py:47
  187.9 5.0 %fusion.60 = bf16[4,512,4,128]{1,3,2,0:T(8,128)(2,1)} fusion(bf16[4,512,4,128]{1,3,2,0:T(8,128)(2,1)} %get-tuple-element.113, s32[]{:T(128)} %get-tuple-element.112, f32[4,512,1024]{1,2,0:T(8,128)} %get-tuple-element.103, f32[4,512]{1,0:T(4,128)S(1)} %get-tuple-element.104, bf16[4,1024,128]{1,2,0:T(8,128)(2,1)S(1)} %get-tuple-element.121), kind=kOutput, calls=%fused_computation.11.clone.1 | convolution fusion | flops 541327360 | bytes 9184256 | tf_op jit(solution)/shard_map/while/body/eval_jaxpr/gqk,kd->qgd/dot_general | solution.py:49
  192.9 7.5 %fusion.59 = (f32[4,512]{1,0:T(4,128)S(1)}, f32[4,512,1024]{1,2,0:T(8,128)}) fusion(pred[512,1024]{0,1:T(8,128)(4,1)} %get-tuple-element.122, bf16[4,512,4,128]{1,3,2,0:T(8,128)(2,1)} %get-tuple-element.124, s32[]{:T(128)} %get-tuple-element.112, bf16[4,1024,128]{1,2,0:T(8,128)(2,1)S(1)} %get-tuple-element.123), kind=kOutput, calls=%fused_computation.37.clone.1 | convolution fusion | flops 545260544 | bytes 9708544 | tf_op jit(solution)/shard_map/while/body/eval_jaxpr/sub | solution.py:47
  200.3 5.0 %fusion.60 = bf16[4,512,4,128]{1,3,2,0:T(8,128)(2,1)} fusion(bf16[4,512,4,128]{1,3,2,0:T(8,128)(2,1)} %get-tuple-element.113, s32[]{:T(128)} %get-tuple-element.112, f32[4,512,1024]{1,2,0:T(8,128)} %get-tuple-element.103, f32[4,512]{1,0:T(4,128)S(1)} %get-tuple-element.104, bf16[4,1024,128]{1,2,0:T(8,128)(2,1)S(1)} %get-tuple-element.121), kind=kOutput, calls=%fused_computation.11.clone.1 | convolution fusion | flops 541327360 | bytes 9184256 | tf_op jit(solution)/shard_map/while/body/eval_jaxpr/gqk,kd->qgd/dot_general | solution.py:49
  205.3 7.5 %fusion.59 = (f32[4,512]{1,0:T(4,128)S(1)}, f32[4,512,1024]{1,2,0:T(8,128)}) fusion(pred[512,1024]{0,1:T(8,128)(4,1)} %get-tuple-element.122, bf16[4,512,4,128]{1,3,2,0:T(8,128)(2,1)} %get-tuple-element.124, s32[]{:T(128)} %get-tuple-element.112, bf16[4,1024,128]{1,2,0:T(8,128)(2,1)S(1)} %get-tuple-element.123), kind=kOutput, calls=%fused_computation.37.clone.1 | convolution fusion | flops 545260544 | bytes 9708544 | tf_op jit(solution)/shard_map/while/body/eval_jaxpr/sub | solution.py:47
  212.8 5.9 %fusion.60 = bf16[4,512,4,128]{1,3,2,0:T(8,128)(2,1)} fusion(bf16[4,512,4,128]{1,3,2,0:T(8,128)(2,1)} %get-tuple-element.113, s32[]{:T(128)} %get-tuple-element.112, f32[4,512,1024]{1,2,0:T(8,128)} %get-tuple-element.103, f32[4,512]{1,0:T(4,128)S(1)} %get-tuple-element.104, bf16[4,1024,128]{1,2,0:T(8,128)(2,1)S(1)} %get-tuple-element.121), kind=kOutput, calls=%fused_computation.11.clone.1 | convolution fusion | flops 541327360 | bytes 9184256 | tf_op jit(solution)/shard_map/while/body/eval_jaxpr/gqk,kd->qgd/dot_general | solution.py:49
  218.7 74.6 %all-gather.6.cloned.1.call-done = bf16[2048,4096]{1,0:T(8,128)(2,1)} async-done(((bf16[2048,256]{1,0:T(8,128)(2,1)}), bf16[2048,4096]{1,0:T(8,128)(2,1)}) %all-gather.6.cloned.1.call-update) | async-done | bytes 16777232 | tf_op jit(solution)/shard_map/all_gather | solution.py:66
  293.3 14.5 %convolution_convert_fusion = bf16[512,4096]{1,0:T(8,128)(2,1)} fusion(bf16[512,2048]{0,1:T(8,128)(2,1)} %bitcast.81, bf16[2048,4096]{1,0:T(8,128)(2,1)} %all-gather.6.cloned.1.call-done), kind=kOutput, calls=%fused_computation.29 | convolution fusion | flops 8592031744 | bytes 23068672 | tf_op jit(solution)/shard_map/dot_general | solution.py:64
  (2 shorter events, 0.0 us)
Async XLA Ops:
  6.5 5.4 %copy-start = (bf16[512,2048]{1,0:T(8,128)(2,1)S(1)}, bf16[512,2048]{1,0:T(8,128)(2,1)}, u32[]{:S(2)}) copy-start(bf16[512,2048]{1,0:T(8,128)(2,1)} %param.7) | copy-start | bytes 6291460
  6.5 80.6 %all-gather.8.cloned.1.call-start = ((), (), s32[]{:S(2)}) async-start(), calls=%async_computation.1 | async-start | bytes 8912896 | tf_op jit(solution)/shard_map/all_gather | solution.py:12
  8.6 153.9 %all-gather.10.cloned.1.call-start = ((), (), s32[]{:S(2)}) async-start(), calls=%async_computation.2 | async-start | bytes 8912896 | tf_op jit(solution)/shard_map/all_gather | solution.py:12
  10.5 282.7 %all-gather.6.cloned.1.call-start = ((), (), s32[]{:S(2)}) async-start(), calls=%async_computation | async-start | bytes 17825792 | tf_op jit(solution)/shard_map/all_gather | solution.py:66
  87.1 4.9 %copy-start.1 = (bf16[512,512]{1,0:T(8,128)(2,1)S(1)}, bf16[512,512]{1,0:T(8,128)(2,1)}, u32[]{:S(2)}) copy-start(bf16[512,512]{1,0:T(8,128)(2,1)} %param.9) | copy-start | bytes 1572868
  162.5 4.9 %copy-start.2 = (bf16[512,512]{1,0:T(8,128)(2,1)S(1)}, bf16[512,512]{1,0:T(8,128)(2,1)}, u32[]{:S(2)}) copy-start(bf16[512,512]{1,0:T(8,128)(2,1)} %param.8) | copy-start | bytes 1572868
Sparse Core Ops, SparseCore 0:
  9.5 77.5 all-gather.7
  89.3 73.1 all-gather.9
  164.6 128.5 all-gather.5
